TPU v7x, 768 devices: a whole 4x8x12 slice. The times are simulated.
768 devices in a mesh: rep: 8 (over y_lo, x), fsdp: 96 (over z, y_hi, core).
Axes of the slice: x: 4, y: 8 (y_hi: 4, y_lo: 2; y = y_hi * 2 + y_lo), z: 12, core: 2. Of those that a mesh axis runs over, the one named last changes fastest.
Arguments:
- block_input: bfloat16 [98304, 4096], P(('rep', 'fsdp')), may hold values from -6 to 6
- ssd_input: bfloat16 [98304, 4096], P(('rep', 'fsdp')), may hold values from -6 to 6
- out_grad: bfloat16 [98304, 4096], P(('rep', 'fsdp')), may hold values from -0.29882812 to 0.29882812
- start_state: bfloat16 [768, 64, 4096], P(('rep', 'fsdp')), may hold values from -12 to 12
- step_bias: float32 [64], replicated, may hold values from -1 to 1
- decay_log: float32 [64], replicated, may hold values from -7 to -2.5
- local_params: float32 [8, 192, 4096], P('rep', 'fsdp'), may hold values from -0.09375 to 0.09375
- global_params: float32 [192, 4096], P('fsdp'), may hold values from -0.75 to 0.75
- momentum: float32 [192, 4096], P('fsdp'), may hold values from -3 to 3
Outputs:
- block_grad: bfloat16 [98304, 4096], P(('rep', 'fsdp'))
- new_params: float32 [192, 4096], P('fsdp')
- new_momentum: float32 [192, 4096], P('fsdp')
All inputs are finite; a program needn't handle non-finite values.
Results may differ from a plain program's by a relative error of at most 0.012.
Values may be sent and summed in bfloat16 or wider, within the bound.
A program may use at most 32 MiB of HBM per device.

v0:
```python
import jax
import jax.numpy as jnp
from jax import lax
from jax.sharding import PartitionSpec as P

HEADS = 64
HEAD_DIM = 64
STATE = 64
BLOCK = 128


inner_rate = 0.002
outer_rate = 0.7
momentum_decay = 0.9


def contract_last(left, right):
    return lax.dot_general(
        left, right, (((1,), (1,)), ((), ())), preferred_element_type=jnp.float32
    )


def ssd_forward(projected, values, carried_in, step_bias, decay_log):
    key_side = projected[:, :STATE]
    query_side = projected[:, STATE : 2 * STATE]
    step_size = jax.nn.softplus(projected[:, 2 * STATE :] + step_bias)
    cumulative = jnp.cumsum(-step_size * jnp.exp(decay_log), axis=0)
    positions = jnp.arange(BLOCK)
    causal = positions[:, None] >= positions[None, :]
    spans = cumulative.T[:, :, None] - cumulative.T[:, None, :]
    decays = jnp.where(causal, jnp.exp(jnp.where(causal, spans, 0.0)), 0.0)
    scores = jnp.dot(query_side, key_side.T, precision=lax.Precision.HIGHEST)
    mixing = scores[None] * decays
    scaled = values.astype(jnp.float32).reshape(BLOCK, HEADS, HEAD_DIM) * step_size[:, :, None]
    within = jnp.einsum("hts,shp->thp", mixing, scaled, precision=lax.Precision.HIGHEST)
    state_f = carried_in.astype(jnp.float32).reshape(HEADS, HEAD_DIM, STATE)
    entering = jnp.einsum("tn,hpn->thp", query_side, state_f, precision=lax.Precision.HIGHEST)
    entering = entering * jnp.exp(cumulative)[:, :, None]
    return (within + entering).reshape(BLOCK, HEADS * HEAD_DIM)


def sequence_grads(projected, ssd_rows, cot_rows, states, step_bias, decay_log):
    blocks = projected.shape[0] // BLOCK

    def single(members):
        proj_one, values, cotangent, carried_in = members
        _, pullback = jax.vjp(
            lambda probe: ssd_forward(probe, values, carried_in, step_bias, decay_log), proj_one
        )
        return pullback(cotangent.astype(jnp.float32))[0]

    grads = lax.map(
        single,
        (
            projected.reshape(blocks, BLOCK, -1),
            ssd_rows.reshape(blocks, BLOCK, -1),
            cot_rows.reshape(blocks, BLOCK, -1),
            states,
        ),
    )
    return grads.reshape(blocks * BLOCK, -1)


def on_device(
    block_input,
    ssd_input,
    out_grad,
    start_state,
    step_bias,
    decay_log,
    local_params,
    global_params,
    momentum,
):
    local_rows = local_params[0]
    weights_shard = local_rows.astype(jnp.bfloat16)
    gathered = lax.all_gather(weights_shard, "fsdp", axis=0, tiled=True)
    projected = contract_last(block_input, gathered)
    proj_grad = sequence_grads(
        projected, ssd_input, out_grad, start_state, step_bias, decay_log
    ).astype(jnp.bfloat16)
    block_grad = jnp.dot(proj_grad, gathered, preferred_element_type=jnp.float32)
    block_grad = block_grad.astype(jnp.bfloat16)
    gradient = lax.psum_scatter(
        lax.dot_general(
            proj_grad, block_input, (((0,), (0,)), ((), ())), preferred_element_type=jnp.float32
        ),
        "fsdp",
        scatter_dimension=0,
        tiled=True,
    )
    pseudo = global_params - (local_rows - inner_rate * gradient)
    mean_pseudo = lax.psum(pseudo.astype(jnp.bfloat16), "rep").astype(jnp.float32) / lax.axis_size(
        "rep"
    )
    new_momentum = momentum_decay * momentum + mean_pseudo
    new_params = global_params - outer_rate * (mean_pseudo + momentum_decay * new_momentum)
    return (block_grad, new_params, new_momentum)


def solution(mesh):
    placed = (
        P(("rep", "fsdp"), None),
        P(("rep", "fsdp"), None),
        P(("rep", "fsdp"), None),
        P(("rep", "fsdp"), None, None),
        P(),
        P(),
        P("rep", "fsdp", None),
        P("fsdp", None),
        P("fsdp", None),
    )
    return jax.shard_map(
        on_device,
        mesh=mesh,
        in_specs=placed,
        out_specs=(P(("rep", "fsdp"), None), P("fsdp", None), P("fsdp", None)),
        check_vma=False,
    )
```

profile of v0, /device:TPU:1, one launch (start us, length us, event | category | flops | bytes accessed | tf_op | source)
XLA Modules:
  0.0 1037.4 jit_solution(18350664095619729653)
XLA Ops:
  7.2 0.0 copy-start
  7.2 0.0 copy-start.5
  7.2 0.0 all-gather.3.cloned.1.call-start
  7.2 1.5 fusion.35
  8.7 0.0 all-gather.3.cloned.1.call-update
  8.8 0.0 all-reduce.6.cloned.1.call-start
  8.8 0.7 exp.27
  9.5 2.3 copy.53
  11.7 2.7 reshape.66
  14.5 0.0 copy-done.5
  14.5 1.6 copy.48
  16.1 0.0 copy-start.9
  16.2 121.0 %all-gather.3.cloned.1.call-done = bf16[96,2,4096]{2,1,0:T(2,128)(2,1)} async-done(((bf16[1,2,4096]{2,1,0:T(2,128)(2,1)}), bf16[96,2,4096]{2,1,0:T(2,128)(2,1)}) %all-gather.3.cloned.1.call-update) | async-done | bytes 1572880 | tf_op jit(solution)/shard_map/all_gather | solution.py:77
  137.2 2.5 reshape.70
  139.7 0.0 copy-done
  139.7 0.6 fusion.38
  140.3 0.3 fusion.29
  140.6 0.0 copy-done.9
  140.6 0.1 negate_multiply_fusion
  140.7 0.1 copy.50
  140.8 0.2 reduce_window_sum.24
  140.9 0.1 copy.56
  141.0 0.1 copy.51
  141.1 0.0 copy-start.3
  141.1 0.0 copy-start.4
  141.1 6.2 fusion.10
  147.3 0.0 copy-done.3
  147.3 0.0 copy-done.4
  147.3 0.0 copy-start.1
  147.3 6.4 fusion.9
  153.8 0.2 fusion.31
  154.0 0.0 copy-done.1
  154.0 1.0 multiply_reduce_fusion
  155.1 0.1 copy.57
  155.2 1.1 reduce_window_sum.25
  156.3 0.1 copy.58
  156.3 0.0 copy-start.2
  156.4 1.5 bitcast_multiply_fusion.2
  157.8 0.1 copy-done.2
  157.9 1.4 convolution_bitcast_fusion
  159.3 0.2 convolution_add_fusion
  159.5 0.1 fusion.23
  159.6 2.3 fusion.37
  161.9 0.0 copy-start.6
  161.9 0.0 copy-start.7
  161.9 0.0 copy-start.8
  161.9 0.0 all-reduce.6.cloned.1.call-update
  161.9 1.3 dynamic-slice.3
  163.9 1.5 convolution_convert_fusion
  165.3 837.5 %all-reduce.6.cloned.1.call-done = f32[192,4096]{1,0:T(8,128)} async-done(((f32[192,4096]{1,0:T(8,128)}), f32[192,4096]{1,0:T(8,128)}) %all-reduce.6.cloned.1.call-update) | async-done | bytes 3145744
  1002.8 0.0 copy-done.6
  1002.8 0.0 copy-done.7
  1002.8 0.9 fusion.27
  1003.7 26.1 %psum.7 = bf16[2,4096]{1,0:T(2,128)(2,1)S(1)} all-reduce(bf16[2,4096]{1,0:T(2,128)(2,1)S(1)} %fusion.27), channel_id=1, replica_groups=mesh['rep'=8,'fsdp'=96] {'rep'}, use_global_device_ids=true, to_apply=%region_8.9 | all-reduce | flops 8192 | bytes 32768 | tf_op jit(solution)/shard_map/psum | solution.py:93
  1029.8 0.0 copy-done.8
  1029.8 0.7 multiply_subtract_fusion
  (2 shorter events, 0.0 us)
Async XLA Ops:
  7.2 132.5 %copy-start = (bf16[128,4096]{1,0:T(8,128)(2,1)S(1)}, bf16[128,4096]{1,0:T(8,128)(2,1)}, u32[]{:S(2)}) copy-start(bf16[128,4096]{1,0:T(8,128)(2,1)} %param.9) | copy-start | bytes 3145732
  7.2 7.3 copy-start.5
  7.2 130.0 %all-gather.3.cloned.1.call-start = ((), (), s32[]{:S(2)}) async-start(), calls=%async_computation | async-start | bytes 1589248 | tf_op jit(solution)/shard_map/all_gather | solution.py:77
  8.8 994.0 %all-reduce.6.cloned.1.call-start = ((), (), s32[]{:S(2)}) async-start(), calls=%async_computation.1 | async-start | bytes 6291456
  16.1 124.4 %copy-start.9 = (f32[64]{0:T(128)S(1)}, f32[64]{0:T(128)}, u32[]{:S(2)}) copy-start(f32[64]{0:T(128)} %param.13) | copy-start | bytes 772
  141.1 6.2 copy-start.3
  141.1 6.2 copy-start.4
  147.3 6.7 copy-start.1
  156.3 1.6 copy-start.2
  161.9 840.9 %copy-start.6 = (f32[1,2,4096]{2,1,0:T(2,128)S(1)}, f32[1,2,4096]{2,1,0:T(2,128)}, u32[]{:S(2)}) copy-start(f32[1,2,4096]{2,1,0:T(2,128)} %param.15) | copy-start | bytes 98308
  161.9 840.9 %copy-start.7 = (f32[2,4096]{1,0:T(2,128)S(1)}, f32[2,4096]{1,0:T(2,128)}, u32[]{:S(2)}) copy-start(f32[2,4096]{1,0:T(2,128)} %param.16) | copy-start | bytes 98308
  161.9 868.0 %copy-start.8 = (f32[2,4096]{1,0:T(2,128)S(1)}, f32[2,4096]{1,0:T(2,128)}, u32[]{:S(2)}) copy-start(f32[2,4096]{1,0:T(2,128)} %param.17) | copy-start | bytes 98308
Sparse Core Ops, SparseCore 0:
  12.2 124.8 all-gather.2
  162.0 840.7 all-reduce.5
where the time goes:
time: 1050 us; the launch traced here: 1040 us
  waiting for transfers between devices  959 us (91%)
  blocking collectives  26.1 us (2%)
  matrix products  20 us (2%)
  between operations  14.9 us (1%)
  local copies, waits for them, and re-layouts  11.6 us (1%)
    unnamed x3, waiting for transfers between devices  838 us
    all_gather x1, waiting for transfers between devices, on_device(): gathered = lax.all_gather(weights_shard, 'fsdp', axis=0, tiled=True)  121 us
    psum x1, blocking collectives, on_device(): lax.psum(pseudo.astype(jnp.bfloat16), 'rep').astype(jnp.float32)  26.1 us
  transfers between devices with their start and end apart: 2, of which 2 were waited for; matrix products, arithmetic and copies ran while one was open for 1% of the time, Pallas kernels for 0%

commit v1 on v0

v1 whole, which is shorter than its diff:
```python
import jax
import jax.numpy as jnp
from jax import lax
from jax.experimental import pallas as pl
from jax.experimental.pallas import tpu as pltpu
from jax.sharding import PartitionSpec as P

HEADS = 64
STATE = 64
BLOCK = 128
D = 4096
COLS = 192
NX, NYL, NYH, NZ, NC = 4, 2, 4, 12, 2
SLICE = D // (NX * NC)
HALF = D // NC
CHUNKS = 4
CHUNK = HALF // CHUNKS
RIGHT, LEFT = 6, 5

inner_rate = 0.002
outer_rate = 0.7
momentum_decay = 0.9

MESH = pl.DeviceIdType.MESH
F32 = jnp.float32
BF16 = jnp.bfloat16
EXACT = lax.Precision.HIGHEST


def place():
    rep = lax.axis_index("rep")
    fsdp = lax.axis_index("fsdp")
    x = lax.rem(rep, NX)
    yl = lax.div(rep, NX)
    z = lax.div(fsdp, NYH * NC)
    yh = lax.rem(lax.div(fsdp, NC), NYH)
    c = lax.rem(fsdp, NC)
    return x, yl, yh, z, c


def device(x, yl, yh, z, c):
    return (yl * NX + x, z * (NYH * NC) + yh * NC + c)


def shift(i, by, n):
    return lax.rem(i + by, n)


def greet(devices):
    barrier = pltpu.get_barrier_semaphore()
    for target in devices:
        pl.semaphore_signal(barrier, inc=1, device_id=target, device_id_type=MESH)
    pl.semaphore_wait(barrier, len(devices))


def replica_group(x, yl, yh, z, c):
    return [
        device(shift(x, dx, NX), shift(yl, dy, NYL), yh, z, shift(c, dc, NC))
        for dx in range(NX)
        for dy in range(NYL)
        for dc in range(NC)
        if (dx, dy, dc) != (0, 0, 0)
    ]


def remote(src, dst, send_sem, recv_sem, target):
    return pltpu.make_async_remote_copy(
        src_ref=src,
        dst_ref=dst,
        send_sem=send_sem,
        recv_sem=recv_sem,
        device_id=target,
        device_id_type=MESH,
    )


def wait_bytes(ref, sem):
    pltpu.make_async_copy(ref, ref, sem).wait()


def gather_kernel(
    rows_ref, input_ref, w_ref, cols_ref, params_ref,
    shards, block32, sem_send, sem_recv, ring_right, ring_left, sem_self,
):
    x, yl, yh, z, c = place()
    me_a = yh * NC + c
    me_q = x * NC + c
    me_r = yl * NX + x
    local = [
        device(x, yl, shift(yh, dy, NYH), z, shift(c, dc, NC))
        for dy in range(NYH)
        for dc in range(NC)
        if (dy, dc) != (0, 0)
    ]
    right = device(x, yl, yh, shift(z, 1, NZ), c)
    left = device(x, yl, yh, shift(z, NZ - 1, NZ), c)
    partner = device(x, yl, yh, z, 1 - c)
    greet(local + [right, left] + replica_group(x, yl, yh, z, c))

    def half(core):
        return pl.ds(pl.multiple_of(core * HALF, HALF), HALF)

    def part(q):
        return pl.ds(pl.multiple_of(q * SLICE, SLICE), SLICE)

    for dy in (2, 1, 3, 0):
        for dc in range(NC):
            core = shift(c, dc, NC)
            src = rows_ref.at[0, :, half(core)]
            dst = shards.at[me_a]
            if (dy, dc) == (0, 0):
                pltpu.make_async_copy(src, dst, sem_recv.at[0]).start()
            else:
                remote(
                    src, dst, sem_send.at[0], sem_recv.at[0],
                    device(x, yl, shift(yh, dy, NYH), z, core),
                ).start()
    for dx in (2, 1, 3, 0):
        for dc in range(NC):
            tx, core = shift(x, dx, NX), shift(c, dc, NC)
            src = input_ref.at[:, part(tx * NC + core)]
            dst = cols_ref.at[me_q]
            if (dx, dc) == (0, 0):
                pltpu.make_async_copy(src, dst, sem_recv.at[1]).start()
            else:
                remote(
                    src, dst, sem_send.at[1], sem_recv.at[1], device(tx, yl, yh, z, core)
                ).start()
    own = yl == c
    for dx in (2, 1, 3, 0):
        for dc in range(NC):
            tx, core = shift(x, dx, NX), shift(c, dc, NC)
            src = rows_ref.at[0, :, part(tx * NC + core)]
            dst = params_ref.at[me_r]
            if (dx, dc) == (0, 0):
                pl.when(own)(pltpu.make_async_copy(src, dst, sem_recv.at[2]).start)
                copy = remote(
                    src, dst, sem_self, sem_recv.at[2], device(tx, 1 - yl, yh, z, core)
                )
                pl.when(jnp.logical_not(own))(copy.start)
            else:
                remote(
                    src, dst, sem_send.at[2], sem_recv.at[2], device(tx, c, yh, z, core)
                ).start()

    wait_bytes(shards, sem_recv.at[0])
    for i in range(NYH * NC):
        block32[2 * i : 2 * i + 2, :] = shards[i]
    w_ref[z, :, half(c)] = block32[...].astype(BF16)

    def chunk(b, k):
        return w_ref.at[b, :, pl.ds(pl.multiple_of(c * HALF + k * CHUNK, CHUNK), CHUNK)]

    def pass_on(b):
        block = w_ref.at[b, :, half(c)]
        remote(block, block, sem_send.at[4], sem_recv.at[3], partner).start()

    for s in range(RIGHT + 1):
        br = shift(z, NZ - s, NZ)
        bl = shift(z, s, NZ)
        for k in range(CHUNKS):
            if s > 0:
                remote(
                    chunk(br, k), chunk(br, k), sem_send.at[3], ring_right.at[s - 1, k], right
                ).wait_recv()
            if s < RIGHT:
                remote(
                    chunk(br, k), chunk(br, k), sem_send.at[3], ring_right.at[s, k], right
                ).start()
            if 0 < s <= LEFT:
                remote(
                    chunk(bl, k), chunk(bl, k), sem_send.at[3], ring_left.at[s - 1, k], left
                ).wait_recv()
            if s < LEFT:
                remote(
                    chunk(bl, k), chunk(bl, k), sem_send.at[3], ring_left.at[s, k], left
                ).start()
        pass_on(br)
        if 0 < s <= LEFT:
            pass_on(bl)

    wait_bytes(cols_ref, sem_recv.at[1])
    wait_bytes(params_ref, sem_recv.at[2])
    wait_bytes(w_ref.at[:, :, half(1 - c)], sem_recv.at[3])
    wait_bytes(shards.at[0:7], sem_send.at[0])
    wait_bytes(cols_ref.at[0:7], sem_send.at[1])
    wait_bytes(params_ref.at[0:7], sem_send.at[2])
    wait_bytes(w_ref.at[0 : RIGHT + LEFT, :, half(c)], sem_send.at[3])
    wait_bytes(w_ref.at[:, :, half(c)], sem_send.at[4])

    @pl.when(jnp.logical_not(own))
    def _():
        wait_bytes(params_ref.at[0], sem_self)


def gather(rows, block_input):
    vmem = pl.BlockSpec(memory_space=pltpu.VMEM)
    hbm = pl.BlockSpec(memory_space=pl.ANY)
    return pl.pallas_call(
        gather_kernel,
        out_shape=(
            jax.ShapeDtypeStruct((NZ, COLS // NZ, D), BF16),
            jax.ShapeDtypeStruct((NX * NC, BLOCK, SLICE), BF16),
            jax.ShapeDtypeStruct((NX * NYL, 2, SLICE), F32),
        ),
        in_specs=[hbm, hbm],
        out_specs=(vmem, vmem, vmem),
        scratch_shapes=[
            pltpu.VMEM((NYH * NC, 2, HALF), F32),
            pltpu.VMEM((COLS // NZ, HALF), F32),
            pltpu.SemaphoreType.DMA((5,)),
            pltpu.SemaphoreType.DMA((4,)),
            pltpu.SemaphoreType.DMA((RIGHT, CHUNKS)),
            pltpu.SemaphoreType.DMA((LEFT, CHUNKS)),
            pltpu.SemaphoreType.DMA,
        ],
        compiler_params=pltpu.CompilerParams(collective_id=0, has_side_effects=True),
        name="gather_rows",
    )(rows, block_input)


def dot(a, b, dims, precision=None):
    return lax.dot_general(
        a, b, ((dims[0], dims[1]), ((), ())), precision=precision, preferred_element_type=F32
    )


NN = ((1,), (0,))
NT = ((1,), (1,))
TN = ((0,), (0,))
GROUP = 8


def block_kernel(
    x_ref, values_ref, cot_ref, state_ref, bias_ref, decay_ref, w_ref,
    out_ref, grad_ref,
    cum_groups, row_groups, both_t, col_t, ds_ref, dq_ref,
):
    proj = dot(x_ref[...], w_ref[...], NT)
    key = proj[:, :STATE]
    query = proj[:, STATE : 2 * STATE]
    raw = proj[:, 2 * STATE :] + bias_ref[...]
    rate = jnp.exp(decay_ref[...])
    step = jnp.maximum(raw, 0.0) + jnp.log1p(jnp.exp(-jnp.abs(raw)))
    t_index = lax.broadcasted_iota(jnp.int32, (BLOCK, BLOCK), 0)
    s_index = lax.broadcasted_iota(jnp.int32, (BLOCK, BLOCK), 1)
    causal = t_index >= s_index
    lower = jnp.where(causal, 1.0, 0.0)
    upper = jnp.where(t_index <= s_index, 1.0, 0.0)
    cum = dot(lower, -step * rate, NN, EXACT)
    both_t[...] = jnp.concatenate([cum, step], axis=1).T
    wide = jnp.concatenate([cum, step], axis=1)
    for g in range(HEADS // GROUP):
        cum_groups[g] = pltpu.roll(wide, (BLOCK - GROUP * g) % BLOCK, 1) if g else wide
    scores = jnp.where(causal, dot(query, key, NT, EXACT), 0.0)
    query_twice = jnp.concatenate([query, query], axis=1)
    ds_ref[...] = jnp.zeros_like(ds_ref)
    dq_ref[...] = jnp.zeros_like(dq_ref)
    first = s_index < STATE
    first16 = lax.broadcasted_iota(jnp.int32, (BLOCK, BLOCK), 1) < STATE
    column = lax.rem(s_index, STATE)
    origin = (s_index - column) + 2 * lax.rem(column, STATE // 2) + lax.div(column, STATE // 2)
    order = jnp.where(t_index == origin, 1.0, 0.0).astype(BF16)
    low = lax.broadcasted_iota(jnp.int32, (STATE // 2, BLOCK), 1) < STATE
    zero_state = jnp.zeros((STATE // 2, BLOCK), BF16)

    @pl.loop(0, HEADS // GROUP)
    def _(g):
        cum_g = cum_groups[g]
        at = pl.multiple_of(g * GROUP, GROUP)
        cum_rows = both_t[pl.ds(at, GROUP), :]
        step_rows = both_t[pl.ds(HEADS + at, GROUP), :]
        rows = jnp.zeros((BLOCK, BLOCK), F32)
        cols = []
        for j in range(GROUP // 2):
            lanes = pl.ds(pl.multiple_of(g * (GROUP * STATE) + j * BLOCK, BLOCK), BLOCK)
            cot = cot_ref[:, lanes]
            val = values_ref[:, lanes]
            zero = jnp.zeros_like(val)
            pair = jnp.concatenate(
                [jnp.where(first16, val, zero), jnp.where(first16, zero, val)], axis=0
            )
            inner = dot(cot, pair, NT)
            sorted_cot = dot(cot, order, NN).astype(BF16)
            states = []
            for e in range(2):
                st = state_ref[g * GROUP + 2 * j + e]
                own = [jnp.where(low, st, zero_state), jnp.where(low, zero_state, st)]
                rest = [zero_state, zero_state]
                states.append(jnp.concatenate(own + rest if e == 0 else rest + own, axis=0))
            entering = dot(sorted_cot, jnp.concatenate(states, axis=1), NN)
            for e in range(2):
                h = 2 * j + e
                cum_t = jnp.broadcast_to(cum_g[:, h : h + 1], (BLOCK, BLOCK))
                decay = jnp.exp(jnp.minimum(cum_t - cum_rows[h : h + 1, :], 0.0))
                a = decay * inner[:, e * BLOCK : (e + 1) * BLOCK]
                step_s = step_rows[h : h + 1, :]
                ds_ref[...] += a * step_s
                b = scores * a
                cols.append(jnp.sum(b, axis=0, keepdims=True))
                w = entering[:, e * BLOCK : (e + 1) * BLOCK] * jnp.exp(cum_t)
                dq_ref[...] += w
                total = jnp.sum(b * step_s + w * query_twice, axis=1, keepdims=True)
                rows = jnp.where(s_index == h, total, rows)
        row_groups[g] = rows
        col_t[pl.ds(at, GROUP), :] = jnp.concatenate(cols, axis=0)

    dcum = row_groups[0]
    for g in range(1, HEADS // GROUP):
        dcum = dcum + pltpu.roll(row_groups[g], GROUP * g, 1)
    dstep = col_t[...].T[:, :HEADS]
    dcum = dcum[:, :HEADS] - step * dstep
    dstep = dstep - rate * dot(upper, dcum, NN, EXACT)
    draw = dstep * jax.nn.sigmoid(raw)
    dscores = jnp.where(causal, ds_ref[...], 0.0)
    dquery = dot(dscores, key, NN, EXACT) + dq_ref[:, :STATE] + dq_ref[:, STATE:]
    dkey = dot(dscores.T, query, NN, EXACT)
    keys = jnp.concatenate([dkey, dquery], axis=1)
    steps = jnp.concatenate([draw, jnp.zeros_like(draw)], axis=1)
    grad_ref[: 2 * STATE, :] = keys.T.astype(BF16)
    grad_ref[2 * STATE :, :] = steps.T[:HEADS, :].astype(BF16)
    keys16 = keys.astype(BF16)
    steps16 = draw.astype(BF16)

    @pl.loop(0, D // 512)
    def _(i):
        lanes = pl.ds(pl.multiple_of(i * 512, 512), 512)
        product = dot(keys16, w_ref[: 2 * STATE, lanes], NN)
        product += dot(steps16, w_ref[2 * STATE :, lanes], NN)
        out_ref[:, lanes] = product.astype(BF16)


def block(block_input, values, cot, state, bias, decay, weights):
    vmem = pl.BlockSpec(memory_space=pltpu.VMEM)
    return pl.pallas_call(
        block_kernel,
        out_shape=(
            jax.ShapeDtypeStruct((BLOCK, D), BF16),
            jax.ShapeDtypeStruct((COLS, BLOCK), BF16),
        ),
        in_specs=[vmem] * 7,
        out_specs=(vmem, vmem),
        scratch_shapes=[
            pltpu.VMEM((HEADS // GROUP, BLOCK, BLOCK), F32),
            pltpu.VMEM((HEADS // GROUP, BLOCK, BLOCK), F32),
            pltpu.VMEM((BLOCK, BLOCK), F32),
            pltpu.VMEM((BLOCK, BLOCK), F32),
            pltpu.VMEM((BLOCK, BLOCK), F32),
            pltpu.VMEM((BLOCK, BLOCK), F32),
        ],
        name="block_backward",
    )(block_input, values, cot, state, bias, decay, weights)


def reduce_kernel(
    grad_ref, cols_ref, params_ref, global_ref, momentum_ref,
    new_params_ref, new_momentum_ref,
    grads, partial, from_z, to_y, from_y, share, shares, sem_send, sem_recv, sem_self,
):
    x, yl, yh, z, c = place()
    y = yh * NYL + yl
    me_q = x * NC + c

    def at_y(i):
        return lax.rem(i, NYL), lax.div(i, NYL)

    along_z = [device(x, yl, yh, shift(z, dz, NZ), c) for dz in range(1, NZ)]
    along_y = []
    for dy in range(1, NYL * NYH):
        tyl, tyh = at_y(shift(y, dy, NYL * NYH))
        along_y.append(device(x, tyl, tyh, z, c))
    greet(along_z + along_y + replica_group(x, yl, yh, z, c))

    def lanes(q):
        return pl.ds(pl.multiple_of(q * BLOCK, BLOCK), BLOCK)

    mine = grads.at[:, lanes(me_q)]
    for dx in (2, 1, 3, 0):
        for dc in range(NC):
            if (dx, dc) == (0, 0):
                pltpu.make_async_copy(grad_ref, mine, sem_recv.at[0]).start()
            else:
                remote(
                    grad_ref, mine, sem_send.at[0], sem_recv.at[0],
                    device(shift(x, dx, NX), yl, yh, z, shift(c, dc, NC)),
                ).start()
    held = params_ref[0]
    for r in range(1, NX * NYL):
        held = held + params_ref[r]
    wait_bytes(grads, sem_recv.at[0])

    products = dot(grads[...], cols_ref[...], NN)
    for b in range(NZ):
        partial[b] = products[16 * b : 16 * b + 16, :].astype(BF16)
    for dz in (6, 5, 7, 4, 8, 3, 9, 2, 10, 1, 11):
        tz = shift(z, dz, NZ)
        remote(
            partial.at[tz], from_z.at[z], sem_send.at[1], sem_recv.at[1],
            device(x, yl, yh, tz, c),
        ).start()
    pltpu.make_async_copy(partial.at[z], from_z.at[z], sem_recv.at[1]).start()
    wait_bytes(from_z, sem_recv.at[1])
    total = from_z[0].astype(F32)
    for b in range(1, NZ):
        total = total + from_z[b].astype(F32)
    for i in range(NYL * NYH):
        to_y[i] = total[2 * i : 2 * i + 2, :]
    for dy in (4, 3, 5, 2, 6, 1, 7):
        ty = shift(y, dy, NYL * NYH)
        tyl, tyh = at_y(ty)
        remote(
            to_y.at[ty], from_y.at[y], sem_send.at[2], sem_recv.at[2],
            device(x, tyl, tyh, z, c),
        ).start()
    pltpu.make_async_copy(to_y.at[y], from_y.at[y], sem_recv.at[2]).start()
    wait_bytes(from_y, sem_recv.at[2])
    summed = from_y[0]
    for i in range(1, NYL * NYH):
        summed = summed + from_y[i]
    share[...] = (inner_rate * summed - held) * (1.0 / (NX * NYL))
    own = yl == c
    for dx in (2, 1, 3, 0):
        for dy in range(NYL):
            tx, tyl = shift(x, dx, NX), shift(yl, dy, NYL)
            dst = shares.at[me_q]
            if (dx, dy) == (0, 0):
                pl.when(own)(pltpu.make_async_copy(share, dst, sem_recv.at[3]).start)
                copy = remote(
                    share, dst, sem_self, sem_recv.at[3], device(tx, tyl, yh, z, 1 - c)
                )
                pl.when(jnp.logical_not(own))(copy.start)
            else:
                remote(
                    share, dst, sem_send.at[3], sem_recv.at[3], device(tx, tyl, yh, z, yl)
                ).start()
    wait_bytes(shares, sem_recv.at[3])
    for q in range(NX * NC):
        cols = slice(q * SLICE, (q + 1) * SLICE)
        outer = global_ref[:, cols]
        mean_pseudo = outer + shares[q]
        momentum = momentum_decay * momentum_ref[:, cols] + mean_pseudo
        new_momentum_ref[:, cols] = momentum
        new_params_ref[:, cols] = outer - outer_rate * (mean_pseudo + momentum_decay * momentum)
    wait_bytes(grads.at[:, : 7 * BLOCK], sem_send.at[0])
    wait_bytes(from_z.at[: NZ - 1], sem_send.at[1])
    wait_bytes(from_y.at[:7], sem_send.at[2])
    wait_bytes(shares.at[:7], sem_send.at[3])

    @pl.when(jnp.logical_not(own))
    def _():
        wait_bytes(share, sem_self)


def reduce(grad, cols, params, global_params, momentum):
    vmem = pl.BlockSpec(memory_space=pltpu.VMEM)
    return pl.pallas_call(
        reduce_kernel,
        out_shape=(
            jax.ShapeDtypeStruct((2, D), F32),
            jax.ShapeDtypeStruct((2, D), F32),
        ),
        in_specs=[vmem] * 5,
        out_specs=(vmem, vmem),
        scratch_shapes=[
            pltpu.VMEM((COLS, NX * NC * BLOCK), BF16),
            pltpu.VMEM((NZ, COLS // NZ, SLICE), BF16),
            pltpu.VMEM((NZ, COLS // NZ, SLICE), BF16),
            pltpu.VMEM((NYL * NYH, 2, SLICE), F32),
            pltpu.VMEM((NYL * NYH, 2, SLICE), F32),
            pltpu.VMEM((2, SLICE), F32),
            pltpu.VMEM((NX * NC, 2, SLICE), F32),
            pltpu.SemaphoreType.DMA((4,)),
            pltpu.SemaphoreType.DMA((4,)),
            pltpu.SemaphoreType.DMA,
        ],
        compiler_params=pltpu.CompilerParams(collective_id=1, has_side_effects=True),
        name="reduce_and_step",
    )(grad, cols, params, global_params, momentum)


def on_device(
    block_input, ssd_input, out_grad, start_state, step_bias, decay_log,
    local_params, global_params, momentum,
):
    weights, cols, params = gather(local_params, block_input)
    block_grad, grad = block(
        block_input,
        ssd_input,
        out_grad,
        start_state.reshape(HEADS, STATE // 2, 2 * STATE),
        step_bias.reshape(1, HEADS),
        decay_log.reshape(1, HEADS),
        weights.reshape(COLS, D),
    )
    new_params, new_momentum = reduce(
        grad, cols.reshape(NX * NC * BLOCK, SLICE), params, global_params, momentum
    )
    return block_grad, new_params, new_momentum


def solution(mesh):
    placed = (
        P(("rep", "fsdp"), None),
        P(("rep", "fsdp"), None),
        P(("rep", "fsdp"), None),
        P(("rep", "fsdp"), None, None),
        P(),
        P(),
        P("rep", "fsdp", None),
        P("fsdp", None),
        P("fsdp", None),
    )
    return jax.shard_map(
        on_device,
        mesh=mesh,
        in_specs=placed,
        out_specs=(P(("rep", "fsdp"), None), P("fsdp", None), P("fsdp", None)),
        check_vma=False,
    )
```

time: 1050 us -> 98.6 us (0.09); the launches traced: 1040 us -> 98.2 us
  waiting for transfers between devices: 959 us -> 0 us
  Pallas kernels: 0 us -> 92.8 us
  blocking collectives: 26.1 us -> 0 us
  matrix products: 20 us -> 0 us
  between operations: 14.9 us -> 0.65 us
    unnamed x3 -> x0, waiting for transfers between devices: 838 us -> none
    all_gather x1 -> x0, waiting for transfers between devices: 121 us -> none  [on_device(): gathered = lax.all_gather(weights_shard, 'fsdp', axis=0, tiled=True)]
    pallas_call x0 -> x3, Pallas kernels: none -> 92.8 us  [the longest x1 47.4 us: gather(): pl.pallas_call(gather_kernel, out_shape=(jax.ShapeDtypeStruct((NZ, COLS /...]
    psum x1 -> x0, blocking collectives: 26.1 us -> none  [on_device(): lax.psum(pseudo.astype(jnp.bfloat16), 'rep').astype(jnp.float32)]
    dot_general x10 -> x0, matrix products: 20 us -> none  [the longest x2 12.6 us: ssd_forward(): jnp.einsum('hts,shp->thp', mixing, scaled, precision=lax.Precision.HIGHEST)]
  transfers between devices with their start and end apart: 2 -> 0, of which waited for: 2 -> 0; matrix products, arithmetic and copies ran while one was open for 1% -> 0% of each run, Pallas kernels for 0% -> 0%
where the time goes in v1:
time: 98.6 us; the launch traced here: 98.2 us
  Pallas kernels  92.8 us (94%)
  local copies, waits for them, and re-layouts  4.69 us (5%)
    pallas_call x1, Pallas kernels, gather(): pl.pallas_call(gather_kernel, out_shape=(jax.ShapeDtypeStruct((NZ, COLS /...  47.4 us
    pallas_call x1, Pallas kernels, reduce(): pl.pallas_call(reduce_kernel, out_shape=(jax.ShapeDtypeStruct((2, D), F32...  31.6 us
    pallas_call x1, Pallas kernels, block(): pl.pallas_call(block_kernel, out_shape=(jax.ShapeDtypeStruct((BLOCK, D),...  13.9 us
    unnamed x3, local copies, waits for them, and re-layouts  4.69 us

profile of v1, /device:TPU:1, one launch (start us, length us, event | category | flops | bytes accessed | tf_op | source)
XLA Modules:
  0.0 98.2 jit_solution(5012911020415310359)
XLA Ops:
  0.6 1.9 %copy.12 = bf16[8,8,32,128]{3,2,1,0:T(8,128)(2,1)} copy(bf16[8,8,32,128]{3,1,2,0:T(8,128)(2,1)} %bitcast.10) | data formatting | bytes 1048576
  2.6 47.4 %gather_rows.1 = (bf16[12,16,4096]{2,1,0:T(8,128)(2,1)}, bf16[8,128,512]{2,1,0:T(8,128)(2,1)}, f32[8,2,512]{2,1,0:T(2,128)}) custom-call(f32[1,2,4096]{2,1,0:T(2,128)} %rows_ref.1, bf16[128,4096]{1,0:T(8,128)(2,1)} %x_ref.1), custom_call_target="tpu_custom_call" | custom-call | tf_op jit(solution)/shard_map/gather_rows/pallas_call | solution.py:199
  50.0 13.9 %block_backward.1 = (bf16[128,4096]{1,0:T(8,128)(2,1)}, bf16[192,128]{1,0:T(8,128)(2,1)}) custom-call(bf16[128,4096]{1,0:T(8,128)(2,1)} %x_ref.1, bf16[128,4096]{1,0:T(8,128)(2,1)} %values_ref.1, bf16[128,4096]{1,0:T(8,128)(2,1)} %cot_ref.1, bf16[64,32,128]{2,1,0:T(8,128)(2,1)} %bitcast.7, f32[1,64]{1,0:T(1,128)} %bitcast.11, f32[1,64]{1,0:T(1,128)} %bitcast.12, ...), custom_call_target="tpu_custom_call" | custom-call | tf_op jit(solution)/shard_map/block_backward/pallas_call | solution.py:335
  63.9 31.6 %reduce_and_step.1 = (f32[2,4096]{1,0:T(2,128)}, f32[2,4096]{1,0:T(2,128)}) custom-call(bf16[192,128]{1,0:T(8,128)(2,1)} %get-tuple-element.12.grad_ref, bf16[1024,512]{1,0:T(8,128)(2,1)} %bitcast.9, f32[8,2,512]{2,1,0:T(2,128)} %get-tuple-element.14.params_ref, f32[2,4096]{1,0:T(2,128)} %global_ref.1, f32[2,4096]{1,0:T(2,128)} %momentum_ref.1), custom_call_target="tpu_custom_call" | custom-call | tf_op jit(solution)/shard_map/reduce_and_step/pallas_call | solution.py:456
  95.4 1.4 %copy.15 = f32[2,4096]{1,0:T(2,128)} copy(f32[2,4096]{1,0:T(2,128)} %get-tuple-element.21) | data formatting | bytes 65536
  96.8 1.4 %copy.16 = f32[2,4096]{1,0:T(2,128)} copy(f32[2,4096]{1,0:T(2,128)} %get-tuple-element.22) | data formatting | bytes 65536

commit v2 on v1

v2 whole, which is shorter than its diff:
```python
import jax
import jax.numpy as jnp
from jax import lax
from jax.experimental import pallas as pl
from jax.experimental.pallas import tpu as pltpu
from jax.sharding import PartitionSpec as P

HEADS = 64
STATE = 64
BLOCK = 128
D = 4096
COLS = 192
NX, NYL, NYH, NZ, NC = 4, 2, 4, 12, 2
SLICE = D // (NX * NC)
HALF = D // NC
CHUNKS = 4
CHUNK = HALF // CHUNKS
RIGHT, LEFT = 6, 5

inner_rate = 0.002
outer_rate = 0.7
momentum_decay = 0.9

MESH = pl.DeviceIdType.MESH
F32 = jnp.float32
BF16 = jnp.bfloat16
EXACT = lax.Precision.HIGHEST


def place():
    rep = lax.axis_index("rep")
    fsdp = lax.axis_index("fsdp")
    x = lax.rem(rep, NX)
    yl = lax.div(rep, NX)
    z = lax.div(fsdp, NYH * NC)
    yh = lax.rem(lax.div(fsdp, NC), NYH)
    c = lax.rem(fsdp, NC)
    return x, yl, yh, z, c


def device(x, yl, yh, z, c):
    return (yl * NX + x, z * (NYH * NC) + yh * NC + c)


def shift(i, by, n):
    return lax.rem(i + by, n)


def replica_group(x, yl, yh, z, c):
    return [
        device(shift(x, dx, NX), shift(yl, dy, NYL), yh, z, shift(c, dc, NC))
        for dx in range(NX)
        for dy in range(NYL)
        for dc in range(NC)
        if (dx, dy, dc) != (0, 0, 0)
    ]


def remote(src, dst, send_sem, recv_sem, target):
    return pltpu.make_async_remote_copy(
        src_ref=src,
        dst_ref=dst,
        send_sem=send_sem,
        recv_sem=recv_sem,
        device_id=target,
        device_id_type=MESH,
    )


def wait_bytes(ref, sem):
    pltpu.make_async_copy(ref, ref, sem).wait()


def dot(a, b, dims, precision=None):
    return lax.dot_general(
        a, b, ((dims[0], dims[1]), ((), ())), precision=precision, preferred_element_type=F32
    )


NN = ((1,), (0,))
NT = ((1,), (1,))
TN = ((0,), (0,))
GROUP = 8

PAIRS = HEADS // 2
EARLY = PAIRS - CHUNKS * (RIGHT + 1)


def step_kernel(
    input_hbm, values_hbm, cot_hbm, state_hbm, bias_hbm, decay_hbm, rows_hbm,
    out_hbm, shares,
    bias_ref, decay_ref, out_ref,
    input_ref, values_ref, cot_ref, state_ref, state32, rows32, rows16, shards, block32,
    w_ref, cols_ref, params_ref, inner_ref, enter_ref,
    cum_groups, row_groups, both_t, col_t, ds_ref, dq_ref,
    mine, grads, partial, from_z, to_y, from_y, share,
    sem_load, sem_send, sem_recv, sem_x, ring_right, ring_left, sem_self,
):
    x, yl, yh, z, c = place()
    y = yh * NYL + yl
    me_a = yh * NC + c
    me_q = x * NC + c
    me_r = yl * NX + x
    own = yl == c

    def at_y(i):
        return lax.rem(i, NYL), lax.div(i, NYL)

    def half(core):
        return pl.ds(pl.multiple_of(core * HALF, HALF), HALF)

    def part(q):
        return pl.ds(pl.multiple_of(q * SLICE, SLICE), SLICE)

    def tokens(q):
        return pl.ds(pl.multiple_of(q * BLOCK, BLOCK), BLOCK)

    def rows_of(b):
        return pl.ds(pl.multiple_of(b * 16, 16), 16)

    loads = [
        pltpu.make_async_copy(src, dst, sem_load.at[i])
        for i, (src, dst) in enumerate(
            [
                (rows_hbm.at[0], rows32),
                (state_hbm.at[0], state_ref),
                (cot_hbm, cot_ref),
                (values_hbm, values_ref),
                (input_hbm, input_ref),
                (bias_hbm, bias_ref),
                (decay_hbm, decay_ref),
            ]
        )
    ]
    for load in loads:
        load.start()

    right = device(x, yl, yh, shift(z, 1, NZ), c)
    left = device(x, yl, yh, shift(z, NZ - 1, NZ), c)
    partner = device(x, yl, yh, z, 1 - c)
    along_z = [device(x, yl, yh, shift(z, dz, NZ), c) for dz in range(1, NZ)]
    along_y = []
    for dy in range(1, NYL * NYH):
        tyl, tyh = at_y(shift(y, dy, NYL * NYH))
        along_y.append(device(x, tyl, tyh, z, c))
    across = [device(x, yl, shift(yh, dy, NYH), z, 1 - c) for dy in range(1, NYH)]
    greeted = along_z + along_y + across + replica_group(x, yl, yh, z, c)
    barrier = pltpu.get_barrier_semaphore()
    for target in greeted:
        pl.semaphore_signal(barrier, inc=1, device_id=target, device_id_type=MESH)
    loads[0].wait()
    rows16[...] = rows32[...].astype(BF16)
    pl.semaphore_wait(barrier, len(greeted))

    for dy in (2, 1, 3, 0):
        for dc in range(NC):
            core = shift(c, dc, NC)
            src = rows16.at[:, half(core)]
            dst = shards.at[me_a]
            if (dy, dc) == (0, 0):
                pltpu.make_async_copy(src, dst, sem_recv.at[0]).start()
            else:
                remote(
                    src, dst, sem_send.at[0], sem_recv.at[0],
                    device(x, yl, shift(yh, dy, NYH), z, core),
                ).start()
    for dx in (2, 1, 3, 0):
        for dc in range(NC):
            tx, core = shift(x, dx, NX), shift(c, dc, NC)
            src = input_hbm.at[:, part(tx * NC + core)]
            dst = cols_ref.at[tokens(me_q)]
            if (dx, dc) == (0, 0):
                pltpu.make_async_copy(src, dst, sem_recv.at[1]).start()
            else:
                remote(
                    src, dst, sem_send.at[1], sem_recv.at[1], device(tx, yl, yh, z, core)
                ).start()
    for dx in (2, 1, 3, 0):
        for dc in range(NC):
            tx, core = shift(x, dx, NX), shift(c, dc, NC)
            src = rows32.at[:, part(tx * NC + core)]
            dst = params_ref.at[me_r]
            if (dx, dc) == (0, 0):
                pl.when(own)(pltpu.make_async_copy(src, dst, sem_recv.at[2]).start)
                copy = remote(
                    src, dst, sem_self.at[0], sem_recv.at[2], device(tx, 1 - yl, yh, z, core)
                )
                pl.when(jnp.logical_not(own))(copy.start)
            else:
                remote(
                    src, dst, sem_send.at[2], sem_recv.at[2], device(tx, c, yh, z, core)
                ).start()

    t_index = lax.broadcasted_iota(jnp.int32, (BLOCK, BLOCK), 0)
    s_index = lax.broadcasted_iota(jnp.int32, (BLOCK, BLOCK), 1)
    first = s_index < STATE
    column = lax.rem(s_index, STATE)
    origin = (s_index - column) + 2 * lax.rem(column, STATE // 2) + lax.div(column, STATE // 2)
    order = jnp.where(t_index == origin, 1.0, 0.0).astype(BF16)
    low = lax.broadcasted_iota(jnp.int32, (STATE // 2, BLOCK), 1) < STATE
    zero_state = jnp.zeros((STATE // 2, BLOCK), BF16)

    def products(p):
        lanes = tokens(p)
        cot = cot_ref[:, lanes]
        val = values_ref[:, lanes]
        zero = jnp.zeros_like(val)
        pair = jnp.concatenate(
            [jnp.where(first, val, zero), jnp.where(first, zero, val)], axis=0
        )
        inner_ref[p] = dot(cot, pair, NT)
        sorted_cot = dot(cot, order, NN).astype(BF16)
        states = []
        for e in range(2):
            st = state32[pl.ds(2 * p + e, STATE // 2, stride=HEADS), :].astype(BF16)
            kept = [jnp.where(low, st, zero_state), jnp.where(low, zero_state, st)]
            rest = [zero_state, zero_state]
            states.append(jnp.concatenate(kept + rest if e == 0 else rest + kept, axis=0))
        enter_ref[p] = dot(sorted_cot, jnp.concatenate(states, axis=1), NN)

    for load in loads[1:]:
        load.wait()
    for j in range(STATE // 2):
        state32[j * HEADS : (j + 1) * HEADS, :] = state_ref[:, j * BLOCK : (j + 1) * BLOCK].astype(F32)
    wait_bytes(shards, sem_recv.at[0])
    for i in range(NYH * NC):
        block32[2 * i : 2 * i + 2, :] = shards[i].astype(F32)
    w_ref[rows_of(z), half(c)] = block32[...].astype(BF16)

    def chunk(b, k):
        return w_ref.at[rows_of(b), pl.ds(pl.multiple_of(c * HALF + k * CHUNK, CHUNK), CHUNK)]

    def pass_on(b):
        block = w_ref.at[rows_of(b), half(c)]
        remote(block, block, sem_send.at[4], sem_recv.at[3], partner).start()

    @pl.loop(0, RIGHT + 1)
    def _(s):
        br = lax.rem(z + NZ - s, NZ)
        bl = lax.rem(z + s, NZ)
        before = jnp.maximum(s - 1, 0)
        for k in range(CHUNKS):
            to_right = chunk(br, k)
            to_left = chunk(bl, k)

            @pl.when(s > 0)
            def _():
                remote(
                    to_right, to_right, sem_send.at[3], ring_right.at[before, k], right
                ).wait_recv()

            @pl.when(s < RIGHT)
            def _():
                remote(
                    to_right, to_right, sem_send.at[3], ring_right.at[s, k], right
                ).start()

            @pl.when(jnp.logical_and(s > 0, s <= LEFT))
            def _():
                remote(
                    to_left, to_left, sem_send.at[3], ring_left.at[before, k], left
                ).wait_recv()

            @pl.when(s < LEFT)
            def _():
                remote(
                    to_left, to_left, sem_send.at[3], ring_left.at[s, k], left
                ).start()

            products(s * CHUNKS + k)

        pass_on(br)

        @pl.when(jnp.logical_and(s > 0, s <= LEFT))
        def _():
            pass_on(bl)

    for p in range(PAIRS - EARLY, PAIRS):
        products(p)
    wait_bytes(w_ref.at[:, half(1 - c)], sem_recv.at[3])

    proj = dot(input_ref[...], w_ref[...], NT)
    key = proj[:, :STATE]
    query = proj[:, STATE : 2 * STATE]
    raw = proj[:, 2 * STATE :] + bias_ref[...]
    rate = jnp.exp(decay_ref[...])
    step = jnp.maximum(raw, 0.0) + jnp.log1p(jnp.exp(-jnp.abs(raw)))
    causal = t_index >= s_index
    lower = jnp.where(causal, 1.0, 0.0)
    upper = jnp.where(t_index <= s_index, 1.0, 0.0)
    cum = dot(lower, -step * rate, NN, EXACT)
    wide = jnp.concatenate([cum, step], axis=1)
    both_t[...] = wide.T
    for g in range(HEADS // GROUP):
        cum_groups[g] = pltpu.roll(wide, (BLOCK - GROUP * g) % BLOCK, 1) if g else wide
    scores = jnp.where(causal, dot(query, key, NT, EXACT), 0.0)
    query_twice = jnp.concatenate([query, query], axis=1)
    ds_ref[...] = jnp.zeros_like(ds_ref)
    dq_ref[...] = jnp.zeros_like(dq_ref)

    @pl.loop(0, HEADS // GROUP)
    def _(g):
        cum_g = cum_groups[g]
        at = pl.multiple_of(g * GROUP, GROUP)
        cum_rows = both_t[pl.ds(at, GROUP), :]
        step_rows = both_t[pl.ds(HEADS + at, GROUP), :]
        rows = jnp.zeros((BLOCK, BLOCK), F32)
        cols = []
        for h in range(GROUP):
            p = g * (GROUP // 2) + h // 2
            lanes = slice((h % 2) * BLOCK, (h % 2 + 1) * BLOCK)
            cum_t = jnp.broadcast_to(cum_g[:, h : h + 1], (BLOCK, BLOCK))
            decay = jnp.exp(jnp.minimum(cum_t - cum_rows[h : h + 1, :], 0.0))
            a = decay * inner_ref[p, :, lanes]
            step_s = step_rows[h : h + 1, :]
            ds_ref[...] += a * step_s
            b = scores * a
            cols.append(jnp.sum(b, axis=0, keepdims=True))
            w = enter_ref[p, :, lanes] * jnp.exp(cum_t)
            dq_ref[...] += w
            total = jnp.sum(b * step_s + w * query_twice, axis=1, keepdims=True)
            rows = jnp.where(s_index == h, total, rows)
        row_groups[g] = rows
        col_t[pl.ds(at, GROUP), :] = jnp.concatenate(cols, axis=0)

    dcum = row_groups[0]
    for g in range(1, HEADS // GROUP):
        dcum = dcum + pltpu.roll(row_groups[g], GROUP * g, 1)
    dstep = col_t[...].T[:, :HEADS]
    dcum = dcum[:, :HEADS] - step * dstep
    dstep = dstep - rate * dot(upper, dcum, NN, EXACT)
    draw = dstep * jax.nn.sigmoid(raw)
    dscores = jnp.where(causal, ds_ref[...], 0.0)
    dquery = dot(dscores, key, NN, EXACT) + dq_ref[:, :STATE] + dq_ref[:, STATE:]
    dkey = dot(dscores.T, query, NN, EXACT)
    keys = jnp.concatenate([dkey, dquery], axis=1)
    steps = jnp.concatenate([draw, jnp.zeros_like(draw)], axis=1)
    mine[: 2 * STATE, :] = keys.T.astype(BF16)
    mine[2 * STATE :, :] = steps.T[:HEADS, :].astype(BF16)

    here = grads.at[:, tokens(me_q)]
    for dx in (2, 1, 3):
        remote(
            mine, here, sem_send.at[5], sem_x.at[dx], device(shift(x, dx, NX), yl, yh, z, c)
        ).start()
    remote(mine, here, sem_send.at[9], sem_recv.at[4], partner).start()
    pltpu.make_async_copy(mine, here, sem_x.at[0]).start()

    keys16 = keys.astype(BF16)
    steps16 = draw.astype(BF16)

    @pl.loop(0, D // 512)
    def _(i):
        lanes = pl.ds(pl.multiple_of(i * 512, 512), 512)
        product = dot(keys16, w_ref[: 2 * STATE, lanes], NN)
        product += dot(steps16, w_ref[2 * STATE :, lanes], NN)
        out_ref[:, lanes] = product.astype(BF16)
        pltpu.make_async_copy(out_ref.at[:, lanes], out_hbm.at[:, lanes], sem_load.at[7]).start()

    for dx in (1, 3, 2):
        there = grads.at[:, tokens(shift(x, NX - dx, NX) * NC + c)]
        copy = remote(there, there, sem_send.at[9], sem_x.at[dx], partner)
        copy.wait_recv()
        remote(there, there, sem_send.at[9], sem_recv.at[4], partner).start()
    wait_bytes(here, sem_x.at[0])
    wait_bytes(cols_ref, sem_recv.at[1])
    wait_bytes(params_ref, sem_recv.at[2])
    held = params_ref[0]
    for r in range(1, NX * NYL):
        held = held + params_ref[r]
    wait_bytes(grads.at[:, : NX * BLOCK], sem_recv.at[4])

    gradient = dot(grads[...], cols_ref[...], NN)
    for b in range(NZ):
        partial[b] = gradient[16 * b : 16 * b + 16, :].astype(BF16)
    for dz in (6, 5, 7, 4, 8, 3, 9, 2, 10, 1, 11):
        tz = shift(z, dz, NZ)
        remote(
            partial.at[tz], from_z.at[z], sem_send.at[6], sem_recv.at[5],
            device(x, yl, yh, tz, c),
        ).start()
    pltpu.make_async_copy(partial.at[z], from_z.at[z], sem_recv.at[5]).start()
    wait_bytes(from_z, sem_recv.at[5])
    total = from_z[0].astype(F32)
    for b in range(1, NZ):
        total = total + from_z[b].astype(F32)
    for i in range(NYL * NYH):
        to_y[i] = total[2 * i : 2 * i + 2, :]
    for dy in (4, 3, 5, 2, 6, 1, 7):
        ty = shift(y, dy, NYL * NYH)
        tyl, tyh = at_y(ty)
        remote(
            to_y.at[ty], from_y.at[y], sem_send.at[7], sem_recv.at[6],
            device(x, tyl, tyh, z, c),
        ).start()
    pltpu.make_async_copy(to_y.at[y], from_y.at[y], sem_recv.at[6]).start()
    wait_bytes(from_y, sem_recv.at[6])
    summed = from_y[0]
    for i in range(1, NYL * NYH):
        summed = summed + from_y[i]
    share[...] = (inner_rate * summed - held) * (1.0 / (NX * NYL))
    for dx in (2, 1, 3, 0):
        for dy in range(NYL):
            tx, tyl = shift(x, dx, NX), shift(yl, dy, NYL)
            dst = shares.at[me_q]
            if (dx, dy) == (0, 0):
                pl.when(own)(pltpu.make_async_copy(share, dst, sem_recv.at[7]).start)
                copy = remote(
                    share, dst, sem_self.at[1], sem_recv.at[7], device(tx, tyl, yh, z, 1 - c)
                )
                pl.when(jnp.logical_not(own))(copy.start)
            else:
                remote(
                    share, dst, sem_send.at[8], sem_recv.at[7], device(tx, tyl, yh, z, yl)
                ).start()
    wait_bytes(shards.at[0:7], sem_send.at[0])
    wait_bytes(cols_ref.at[0 : 7 * BLOCK], sem_send.at[1])
    wait_bytes(params_ref.at[0:7], sem_send.at[2])
    wait_bytes(w_ref.at[0 : 16 * (RIGHT + LEFT), half(c)], sem_send.at[3])
    wait_bytes(w_ref.at[:, half(c)], sem_send.at[4])
    wait_bytes(grads.at[:, : 3 * BLOCK], sem_send.at[5])
    wait_bytes(grads.at[:, : NX * BLOCK], sem_send.at[9])
    wait_bytes(from_z.at[: NZ - 1], sem_send.at[6])
    wait_bytes(from_y.at[:7], sem_send.at[7])

    @pl.when(jnp.logical_not(own))
    def _():
        wait_bytes(params_ref.at[0], sem_self.at[0])
        wait_bytes(share, sem_self.at[1])

    wait_bytes(out_ref, sem_load.at[7])
    wait_bytes(shares, sem_recv.at[7])
    wait_bytes(shares.at[:7], sem_send.at[8])


def step(block_input, values, cot, state, bias, decay, rows):
    vmem = pl.BlockSpec(memory_space=pltpu.VMEM)
    hbm = pl.BlockSpec(memory_space=pl.ANY)
    square = pltpu.VMEM((BLOCK, BLOCK), F32)
    groups = pltpu.VMEM((HEADS // GROUP, BLOCK, BLOCK), F32)
    return pl.pallas_call(
        step_kernel,
        out_shape=(
            jax.ShapeDtypeStruct((BLOCK, D), BF16),
            jax.ShapeDtypeStruct((NX * NC, 2, SLICE), F32),
        ),
        in_specs=[hbm] * 7,
        out_specs=(hbm, vmem),
        scratch_shapes=[
            pltpu.VMEM((1, HEADS), F32),
            pltpu.VMEM((1, HEADS), F32),
            pltpu.VMEM((BLOCK, D), BF16),
            pltpu.VMEM((BLOCK, D), BF16),
            pltpu.VMEM((BLOCK, D), BF16),
            pltpu.VMEM((BLOCK, D), BF16),
            pltpu.VMEM((HEADS, D), BF16),
            pltpu.VMEM((HEADS * STATE // 2, BLOCK), F32),
            pltpu.VMEM((2, D), F32),
            pltpu.VMEM((2, D), BF16),
            pltpu.VMEM((NYH * NC, 2, HALF), BF16),
            pltpu.VMEM((COLS // NZ, HALF), F32),
            pltpu.VMEM((COLS, D), BF16),
            pltpu.VMEM((NX * NC * BLOCK, SLICE), BF16),
            pltpu.VMEM((NX * NYL, 2, SLICE), F32),
            pltpu.VMEM((PAIRS, BLOCK, 2 * BLOCK), F32),
            pltpu.VMEM((PAIRS, BLOCK, 2 * BLOCK), F32),
            groups,
            groups,
            square,
            pltpu.VMEM((HEADS, BLOCK), F32),
            square,
            square,
            pltpu.VMEM((COLS, BLOCK), BF16),
            pltpu.VMEM((COLS, NX * NC * BLOCK), BF16),
            pltpu.VMEM((NZ, COLS // NZ, SLICE), BF16),
            pltpu.VMEM((NZ, COLS // NZ, SLICE), BF16),
            pltpu.VMEM((NYL * NYH, 2, SLICE), F32),
            pltpu.VMEM((NYL * NYH, 2, SLICE), F32),
            pltpu.VMEM((2, SLICE), F32),
            pltpu.SemaphoreType.DMA((8,)),
            pltpu.SemaphoreType.DMA((10,)),
            pltpu.SemaphoreType.DMA((8,)),
            pltpu.SemaphoreType.DMA((NX,)),
            pltpu.SemaphoreType.DMA((RIGHT, CHUNKS)),
            pltpu.SemaphoreType.DMA((LEFT, CHUNKS)),
            pltpu.SemaphoreType.DMA((2,)),
        ],
        compiler_params=pltpu.CompilerParams(
            collective_id=0, has_side_effects=True, vmem_limit_bytes=62 << 20
        ),
        name="block_step",
    )(block_input, values, cot, state, bias, decay, rows)


def outer_kernel(
    grad_hbm, shares_ref, global_ref, momentum_ref,
    out_hbm, new_params_ref, new_momentum_ref, held, sem_in, sem_out,
):
    width = D // 4
    cuts = [slice(i * width, (i + 1) * width) for i in range(4)]
    takes = [
        pltpu.make_async_copy(grad_hbm.at[:, cut], held.at[:, cut], sem_in.at[i])
        for i, cut in enumerate(cuts)
    ]
    gives = [
        pltpu.make_async_copy(held.at[:, cut], out_hbm.at[:, cut], sem_out.at[i])
        for i, cut in enumerate(cuts)
    ]
    for take in takes:
        take.start()
    for take, give in zip(takes, gives):
        take.wait()
        give.start()
    for q in range(NX * NC):
        cols = slice(q * SLICE, (q + 1) * SLICE)
        outer = global_ref[:, cols]
        mean_pseudo = outer + shares_ref[q]
        momentum = momentum_decay * momentum_ref[:, cols] + mean_pseudo
        new_momentum_ref[:, cols] = momentum
        new_params_ref[:, cols] = outer - outer_rate * (mean_pseudo + momentum_decay * momentum)
    for give in gives:
        give.wait()


def outer(grad, shares, global_params, momentum):
    vmem = pl.BlockSpec(memory_space=pltpu.VMEM)
    hbm = pl.BlockSpec(memory_space=pl.ANY)
    return pl.pallas_call(
        outer_kernel,
        out_shape=(
            jax.ShapeDtypeStruct((BLOCK, D), BF16),
            jax.ShapeDtypeStruct((2, D), F32),
            jax.ShapeDtypeStruct((2, D), F32),
        ),
        in_specs=[hbm, vmem, vmem, vmem],
        out_specs=(hbm, vmem, vmem),
        scratch_shapes=[
            pltpu.VMEM((BLOCK, D), BF16),
            pltpu.SemaphoreType.DMA((4,)),
            pltpu.SemaphoreType.DMA((4,)),
        ],
        compiler_params=pltpu.CompilerParams(vmem_limit_bytes=62 << 20),
        name="outer_step",
    )(grad, shares, global_params, momentum)


def on_device(
    block_input, ssd_input, out_grad, start_state, step_bias, decay_log,
    local_params, global_params, momentum,
):
    grad, shares = step(
        block_input,
        ssd_input,
        out_grad,
        start_state,
        step_bias.reshape(1, HEADS),
        decay_log.reshape(1, HEADS),
        local_params,
    )
    return outer(grad, shares, global_params, momentum)


def solution(mesh):
    placed = (
        P(("rep", "fsdp"), None),
        P(("rep", "fsdp"), None),
        P(("rep", "fsdp"), None),
        P(("rep", "fsdp"), None, None),
        P(),
        P(),
        P("rep", "fsdp", None),
        P("fsdp", None),
        P("fsdp", None),
    )
    return jax.shard_map(
        on_device,
        mesh=mesh,
        in_specs=placed,
        out_specs=(P(("rep", "fsdp"), None), P("fsdp", None), P("fsdp", None)),
        check_vma=False,
    )
```

time: 98.6 us -> 83.8 us (0.85)
  Pallas kernels: 92.8 us -> 82.9 us
  local copies, waits for them, and re-layouts: 4.69 us -> 0 us
    pallas_call x3 -> x2, Pallas kernels: 92.8 us -> 82.9 us  [the longest x1 79.5 us: step(): pl.pallas_call(step_kernel, out_shape=(jax.ShapeDtypeStruct((BLOCK, D), B...]
    unnamed x3 -> x0, local copies, waits for them, and re-layouts: 4.69 us -> none
where the time goes in v2:
time: 83.8 us; the launch traced here: 83.5 us
  Pallas kernels  82.9 us (99%)
    pallas_call x1, Pallas kernels, step(): pl.pallas_call(step_kernel, out_shape=(jax.ShapeDtypeStruct((BLOCK, D), B...  79.5 us
    pallas_call x1, Pallas kernels, outer(): pl.pallas_call(outer_kernel, out_shape=(jax.ShapeDtypeStruct((BLOCK, D),...  3.4 us

profile of v2, /device:TPU:1, one launch (start us, length us, event | category | flops | bytes accessed | tf_op | source)
XLA Modules:
  0.0 83.5 jit_solution(15204933493403690285)
XLA Ops:
  0.6 79.5 %block_step.1 = (bf16[128,4096]{1,0:T(8,128)(2,1)}, f32[8,2,512]{2,1,0:T(2,128)}) custom-call(bf16[128,4096]{1,0:T(8,128)(2,1)} %input_hbm.1, bf16[128,4096]{1,0:T(8,128)(2,1)} %values_hbm.1, bf16[128,4096]{1,0:T(8,128)(2,1)} %cot_hbm.1, bf16[1,64,4096]{2,1,0:T(8,128)(2,1)} %state_hbm.1, f32[1,64]{1,0:T(1,128)} %bitcast.2, f32[1,64]{1,0:T(1,128)} %bitcast.3, ...), custom_call_target="tpu_custom_call" | custom-call | tf_op jit(solution)/shard_map/block_step/pallas_call | solution.py:441
  80.1 3.4 %outer_step.1 = (bf16[128,4096]{1,0:T(8,128)(2,1)}, f32[2,4096]{1,0:T(2,128)}, f32[2,4096]{1,0:T(2,128)}) custom-call(bf16[128,4096]{1,0:T(8,128)(2,1)} %get-tuple-element.5.grad_hbm, f32[8,2,512]{2,1,0:T(2,128)} %get-tuple-element.6.shares_ref, f32[2,4096]{1,0:T(2,128)} %global_ref.1, f32[2,4096]{1,0:T(2,128)} %momentum_ref.1), custom_call_target="tpu_custom_call" | custom-call | tf_op jit(solution)/shard_map/outer_step/pallas_call | solution.py:528

commit v3 on v2

--- a/solution.py
+++ b/solution.py
@@ -15,7 +15,7 @@
 HALF = D // NC
 CHUNKS = 4
 CHUNK = HALF // CHUNKS
-RIGHT, LEFT = 6, 5
+STAGES = 3
 
 inner_rate = 0.002
 outer_rate = 0.7
@@ -83,7 +83,7 @@
 GROUP = 8
 
 PAIRS = HEADS // 2
-EARLY = PAIRS - CHUNKS * (RIGHT + 1)
+EARLY = PAIRS - 2 * CHUNKS * STAGES
 
 
 def step_kernel(
@@ -137,6 +137,8 @@
 
     right = device(x, yl, yh, shift(z, 1, NZ), c)
     left = device(x, yl, yh, shift(z, NZ - 1, NZ), c)
+    right2 = device(x, yl, yh, shift(z, 2, NZ), c)
+    left2 = device(x, yl, yh, shift(z, NZ - 2, NZ), c)
     partner = device(x, yl, yh, z, 1 - c)
     along_z = [device(x, yl, yh, shift(z, dz, NZ), c) for dz in range(1, NZ)]
     along_y = []
@@ -222,6 +224,8 @@
         load.wait()
     for j in range(STATE // 2):
         state32[j * HEADS : (j + 1) * HEADS, :] = state_ref[:, j * BLOCK : (j + 1) * BLOCK].astype(F32)
+    for p in range(PAIRS - EARLY, PAIRS):
+        products(p)
     wait_bytes(shards, sem_recv.at[0])
     for i in range(NYH * NC):
         block32[2 * i : 2 * i + 2, :] = shards[i].astype(F32)
@@ -234,49 +238,56 @@
         block = w_ref.at[rows_of(b), half(c)]
         remote(block, block, sem_send.at[4], sem_recv.at[3], partner).start()
 
-    @pl.loop(0, RIGHT + 1)
+    def hop(b, k, sem, target):
+        piece = chunk(b, k)
+        return remote(piece, piece, sem_send.at[3], sem, target)
+
+    @pl.loop(0, STAGES)
     def _(s):
-        br = lax.rem(z + NZ - s, NZ)
-        bl = lax.rem(z + s, NZ)
-        before = jnp.maximum(s - 1, 0)
+        br = lax.rem(z + NZ - 2 * s, NZ)
+        bl = lax.rem(z + 2 * s, NZ)
         for k in range(CHUNKS):
-            to_right = chunk(br, k)
-            to_left = chunk(bl, k)
-
-            @pl.when(s > 0)
-            def _():
-                remote(
-                    to_right, to_right, sem_send.at[3], ring_right.at[before, k], right
-                ).wait_recv()
-
-            @pl.when(s < RIGHT)
-            def _():
-                remote(
-                    to_right, to_right, sem_send.at[3], ring_right.at[s, k], right
-                ).start()
-
-            @pl.when(jnp.logical_and(s > 0, s <= LEFT))
-            def _():
-                remote(
-                    to_left, to_left, sem_send.at[3], ring_left.at[before, k], left
-                ).wait_recv()
-
-            @pl.when(s < LEFT)
-            def _():
-                remote(
-                    to_left, to_left, sem_send.at[3], ring_left.at[s, k], left
-                ).start()
-
-            products(s * CHUNKS + k)
+            pl.when(s > 0)(hop(br, k, ring_right.at[2 * s, k], right).wait_recv)
+            if k < CHUNKS // 2:
+                hop(br, k, ring_right.at[2 * s + 2, k], right2).start()
+            else:
+                pl.when(s < STAGES - 1)(hop(br, k, ring_right.at[2 * s + 2, k], right2).start)
+            hop(br, k, ring_right.at[2 * s + 1, k], right).start()
+            pl.when(s > 0)(hop(bl, k, ring_left.at[2 * s, k], left).wait_recv)
+            if k >= CHUNKS // 2:
+                hop(bl, k, ring_left.at[2 * s + 2, k], left2).start()
+            else:
+                pl.when(s < STAGES - 1)(hop(bl, k, ring_left.at[2 * s + 2, k], left2).start)
+            hop(bl, k, ring_left.at[2 * s + 1, k], left).start()
+            products(s * 2 * CHUNKS + 2 * k)
+            products(s * 2 * CHUNKS + 2 * k + 1)
 
         pass_on(br)
 
-        @pl.when(jnp.logical_and(s > 0, s <= LEFT))
+        @pl.when(s > 0)
         def _():
             pass_on(bl)
-
-    for p in range(PAIRS - EARLY, PAIRS):
-        products(p)
+            fr = lax.rem(z + NZ + 1 - 2 * s, NZ)
+            fl = lax.rem(z + 2 * s - 1, NZ)
+            for k in range(CHUNKS):
+                hop(fr, k, ring_right.at[2 * s - 1, k], right).wait_recv()
+            pass_on(fr)
+            for k in range(CHUNKS):
+                hop(fl, k, ring_left.at[2 * s - 1, k], left).wait_recv()
+            pass_on(fl)
+
+    last = 2 * STAGES - 1
+    fr, fl, far = shift(z, NZ - last, NZ), shift(z, last, NZ), shift(z, NZ // 2, NZ)
+    for k in range(CHUNKS):
+        hop(fr, k, ring_right.at[last, k], right).wait_recv()
+    pass_on(fr)
+    for k in range(CHUNKS):
+        hop(fl, k, ring_left.at[last, k], left).wait_recv()
+    pass_on(fl)
+    for k in range(CHUNKS):
+        ring = ring_right if k < CHUNKS // 2 else ring_left
+        hop(far, k, ring.at[last + 1, k], right).wait_recv()
+    pass_on(far)
     wait_bytes(w_ref.at[:, half(1 - c)], sem_recv.at[3])
 
     proj = dot(input_ref[...], w_ref[...], NT)
@@ -416,7 +427,7 @@
     wait_bytes(shards.at[0:7], sem_send.at[0])
     wait_bytes(cols_ref.at[0 : 7 * BLOCK], sem_send.at[1])
     wait_bytes(params_ref.at[0:7], sem_send.at[2])
-    wait_bytes(w_ref.at[0 : 16 * (RIGHT + LEFT), half(c)], sem_send.at[3])
+    wait_bytes(w_ref.at[0 : 16 * (NZ - 1), half(c)], sem_send.at[3])
     wait_bytes(w_ref.at[:, half(c)], sem_send.at[4])
     wait_bytes(grads.at[:, : 3 * BLOCK], sem_send.at[5])
     wait_bytes(grads.at[:, : NX * BLOCK], sem_send.at[9])
@@ -481,8 +492,8 @@
             pltpu.SemaphoreType.DMA((10,)),
             pltpu.SemaphoreType.DMA((8,)),
             pltpu.SemaphoreType.DMA((NX,)),
-            pltpu.SemaphoreType.DMA((RIGHT, CHUNKS)),
-            pltpu.SemaphoreType.DMA((LEFT, CHUNKS)),
+            pltpu.SemaphoreType.DMA((2 * STAGES + 1, CHUNKS)),
+            pltpu.SemaphoreType.DMA((2 * STAGES + 1, CHUNKS)),
             pltpu.SemaphoreType.DMA((2,)),
         ],
         compiler_params=pltpu.CompilerParams(
@@ -493,11 +504,18 @@
 
 
 def outer_kernel(
-    grad_hbm, shares_ref, global_ref, momentum_ref,
-    out_hbm, new_params_ref, new_momentum_ref, held, sem_in, sem_out,
+    grad_hbm, shares_hbm, global_hbm, momentum_hbm,
+    out_hbm, new_params_hbm, new_momentum_hbm,
+    held, shares_ref, global_ref, momentum_ref, new_params_ref, new_momentum_ref, sem_in, sem_out,
 ):
     width = D // 4
     cuts = [slice(i * width, (i + 1) * width) for i in range(4)]
+    small = [
+        pltpu.make_async_copy(src, dst, sem_in.at[4 + i])
+        for i, (src, dst) in enumerate(
+            [(shares_hbm, shares_ref), (global_hbm, global_ref), (momentum_hbm, momentum_ref)]
+        )
+    ]
     takes = [
         pltpu.make_async_copy(grad_hbm.at[:, cut], held.at[:, cut], sem_in.at[i])
         for i, cut in enumerate(cuts)
@@ -506,11 +524,14 @@
         pltpu.make_async_copy(held.at[:, cut], out_hbm.at[:, cut], sem_out.at[i])
         for i, cut in enumerate(cuts)
     ]
-    for take in takes:
+    results = [
+        pltpu.make_async_copy(new_params_ref, new_params_hbm, sem_out.at[4]),
+        pltpu.make_async_copy(new_momentum_ref, new_momentum_hbm, sem_out.at[5]),
+    ]
+    for take in small + takes:
         take.start()
-    for take, give in zip(takes, gives):
+    for take in small:
         take.wait()
-        give.start()
     for q in range(NX * NC):
         cols = slice(q * SLICE, (q + 1) * SLICE)
         outer = global_ref[:, cols]
@@ -518,13 +539,18 @@
         momentum = momentum_decay * momentum_ref[:, cols] + mean_pseudo
         new_momentum_ref[:, cols] = momentum
         new_params_ref[:, cols] = outer - outer_rate * (mean_pseudo + momentum_decay * momentum)
-    for give in gives:
+    for result in results:
+        result.start()
+    for take, give in zip(takes, gives):
+        take.wait()
+        give.start()
+    for give in gives + results:
         give.wait()
 
 
 def outer(grad, shares, global_params, momentum):
-    vmem = pl.BlockSpec(memory_space=pltpu.VMEM)
     hbm = pl.BlockSpec(memory_space=pl.ANY)
+    rows = pltpu.VMEM((2, D), F32)
     return pl.pallas_call(
         outer_kernel,
         out_shape=(
@@ -532,12 +558,17 @@
             jax.ShapeDtypeStruct((2, D), F32),
             jax.ShapeDtypeStruct((2, D), F32),
         ),
-        in_specs=[hbm, vmem, vmem, vmem],
-        out_specs=(hbm, vmem, vmem),
+        in_specs=[hbm] * 4,
+        out_specs=(hbm, hbm, hbm),
         scratch_shapes=[
             pltpu.VMEM((BLOCK, D), BF16),
-            pltpu.SemaphoreType.DMA((4,)),
-            pltpu.SemaphoreType.DMA((4,)),
+            pltpu.VMEM((NX * NC, 2, SLICE), F32),
+            rows,
+            rows,
+            rows,
+            rows,
+            pltpu.SemaphoreType.DMA((7,)),
+            pltpu.SemaphoreType.DMA((6,)),
         ],
         compiler_params=pltpu.CompilerParams(vmem_limit_bytes=62 << 20),
         name="outer_step",

time: 83.8 us -> 76.8 us (0.916)
  Pallas kernels: 82.9 us -> 76 us
    pallas_call x1, Pallas kernels: 79.5 us -> 74 us  [step(): pl.pallas_call(step_kernel, out_shape=(jax.ShapeDtypeStruct((BLOCK, D), B...]
    pallas_call x1, Pallas kernels: 3.4 us -> 2.09 us  [outer(): pl.pallas_call(outer_kernel, out_shape=(jax.ShapeDtypeStruct((BLOCK, D),...]
where the time goes in v3:
time: 76.8 us; the launch traced here: 76.7 us
  Pallas kernels  76 us (99%)
    pallas_call x1, Pallas kernels, step(): pl.pallas_call(step_kernel, out_shape=(jax.ShapeDtypeStruct((BLOCK, D), B...  74 us
    pallas_call x1, Pallas kernels, outer(): pl.pallas_call(outer_kernel, out_shape=(jax.ShapeDtypeStruct((BLOCK, D),...  2.09 us

profile of v3, /device:TPU:1, one launch (start us, length us, event | category | flops | bytes accessed | tf_op | source)
XLA Modules:
  0.0 76.7 jit_solution(409366106002999716)
XLA Ops:
  0.6 74.0 %block_step.1 = (bf16[128,4096]{1,0:T(8,128)(2,1)}, f32[8,2,512]{2,1,0:T(2,128)}) custom-call(bf16[128,4096]{1,0:T(8,128)(2,1)} %input_hbm.1, bf16[128,4096]{1,0:T(8,128)(2,1)} %values_hbm.1, bf16[128,4096]{1,0:T(8,128)(2,1)} %cot_hbm.1, bf16[1,64,4096]{2,1,0:T(8,128)(2,1)} %state_hbm.1, f32[1,64]{1,0:T(1,128)} %bitcast.2, f32[1,64]{1,0:T(1,128)} %bitcast.3, ...), custom_call_target="tpu_custom_call" | custom-call | tf_op jit(solution)/shard_map/block_step/pallas_call | solution.py:452
  74.6 2.1 %outer_step.1 = (bf16[128,4096]{1,0:T(8,128)(2,1)}, f32[2,4096]{1,0:T(2,128)}, f32[2,4096]{1,0:T(2,128)}) custom-call(bf16[128,4096]{1,0:T(8,128)(2,1)} %get-tuple-element.5.grad_hbm, f32[8,2,512]{2,1,0:T(2,128)} %get-tuple-element.6.shares_hbm, f32[2,4096]{1,0:T(2,128)} %global_hbm.1, f32[2,4096]{1,0:T(2,128)} %momentum_hbm.1), custom_call_target="tpu_custom_call" | custom-call | tf_op jit(solution)/shard_map/outer_step/pallas_call | solution.py:554

commit v4 on v3

--- a/solution.py
+++ b/solution.py
@@ -81,6 +81,9 @@
 NT = ((1,), (1,))
 TN = ((0,), (0,))
 GROUP = 8
+ROWS = 128
+BY_LANES = (2, 6)
+LOG2E = 1.4426950408889634
 
 PAIRS = HEADS // 2
 EARLY = PAIRS - 2 * CHUNKS * STAGES
@@ -92,7 +95,7 @@
     bias_ref, decay_ref, out_ref,
     input_ref, values_ref, cot_ref, state_ref, state32, rows32, rows16, shards, block32,
     w_ref, cols_ref, params_ref, inner_ref, enter_ref,
-    cum_groups, row_groups, both_t, col_t, ds_ref, dq_ref,
+    cum_groups, row_groups, both_t, col_t, ds_ref, dq_ref, scores_ref, query_ref, pick_ref,
     mine, grads, partial, from_z, to_y, from_y, share,
     sem_load, sem_send, sem_recv, sem_x, ring_right, ring_left, sem_self,
 ):
@@ -259,8 +262,6 @@
             else:
                 pl.when(s < STAGES - 1)(hop(bl, k, ring_left.at[2 * s + 2, k], left2).start)
             hop(bl, k, ring_left.at[2 * s + 1, k], left).start()
-            products(s * 2 * CHUNKS + 2 * k)
-            products(s * 2 * CHUNKS + 2 * k + 1)
 
         pass_on(br)
 
@@ -275,6 +276,9 @@
             for k in range(CHUNKS):
                 hop(fl, k, ring_left.at[2 * s - 1, k], left).wait_recv()
             pass_on(fl)
+
+        for i in range(2 * CHUNKS):
+            products(s * 2 * CHUNKS + i)
 
     last = 2 * STAGES - 1
     fr, fl, far = shift(z, NZ - last, NZ), shift(z, last, NZ), shift(z, NZ // 2, NZ)
@@ -288,9 +292,9 @@
         ring = ring_right if k < CHUNKS // 2 else ring_left
         hop(far, k, ring.at[last + 1, k], right).wait_recv()
     pass_on(far)
+    proj = dot(input_ref[:, half(c)], w_ref[:, half(c)], NT)
     wait_bytes(w_ref.at[:, half(1 - c)], sem_recv.at[3])
-
-    proj = dot(input_ref[...], w_ref[...], NT)
+    proj = proj + dot(input_ref[:, half(1 - c)], w_ref[:, half(1 - c)], NT)
     key = proj[:, :STATE]
     query = proj[:, STATE : 2 * STATE]
     raw = proj[:, 2 * STATE :] + bias_ref[...]
@@ -300,39 +304,61 @@
     lower = jnp.where(causal, 1.0, 0.0)
     upper = jnp.where(t_index <= s_index, 1.0, 0.0)
     cum = dot(lower, -step * rate, NN, EXACT)
-    wide = jnp.concatenate([cum, step], axis=1)
+    wide = jnp.concatenate([cum * LOG2E, step], axis=1)
     both_t[...] = wide.T
     for g in range(HEADS // GROUP):
         cum_groups[g] = pltpu.roll(wide, (BLOCK - GROUP * g) % BLOCK, 1) if g else wide
-    scores = jnp.where(causal, dot(query, key, NT, EXACT), 0.0)
-    query_twice = jnp.concatenate([query, query], axis=1)
+    scores_ref[...] = jnp.where(causal, dot(query, key, NT, EXACT), 0.0)
+    query_ref[...] = jnp.concatenate([query, query], axis=1)
+    by_product = [h for h in range(GROUP) if h not in BY_LANES for _ in range(2)]
+    for i, h in enumerate(by_product):
+        pick_ref[i * BLOCK : (i + 1) * BLOCK, :] = jnp.where(s_index == h, 1.0, 0.0).astype(BF16)
+    lane_index = lax.broadcasted_iota(jnp.int32, (ROWS, BLOCK), 1)
     ds_ref[...] = jnp.zeros_like(ds_ref)
     dq_ref[...] = jnp.zeros_like(dq_ref)
 
     @pl.loop(0, HEADS // GROUP)
     def _(g):
-        cum_g = cum_groups[g]
         at = pl.multiple_of(g * GROUP, GROUP)
         cum_rows = both_t[pl.ds(at, GROUP), :]
         step_rows = both_t[pl.ds(HEADS + at, GROUP), :]
-        rows = jnp.zeros((BLOCK, BLOCK), F32)
-        cols = []
-        for h in range(GROUP):
-            p = g * (GROUP // 2) + h // 2
-            lanes = slice((h % 2) * BLOCK, (h % 2 + 1) * BLOCK)
-            cum_t = jnp.broadcast_to(cum_g[:, h : h + 1], (BLOCK, BLOCK))
-            decay = jnp.exp(jnp.minimum(cum_t - cum_rows[h : h + 1, :], 0.0))
-            a = decay * inner_ref[p, :, lanes]
-            step_s = step_rows[h : h + 1, :]
-            ds_ref[...] += a * step_s
-            b = scores * a
-            cols.append(jnp.sum(b, axis=0, keepdims=True))
-            w = enter_ref[p, :, lanes] * jnp.exp(cum_t)
-            dq_ref[...] += w
-            total = jnp.sum(b * step_s + w * query_twice, axis=1, keepdims=True)
-            rows = jnp.where(s_index == h, total, rows)
-        row_groups[g] = rows
-        col_t[pl.ds(at, GROUP), :] = jnp.concatenate(cols, axis=0)
+        cols = [jnp.zeros((8, BLOCK), F32) for _ in range(GROUP)]
+        for r in range(0, BLOCK, ROWS):
+            block = slice(r, r + ROWS)
+            cum_g = cum_groups[g, block, :]
+            score = scores_ref[block, :]
+            twice = query_ref[block, :]
+            ds = ds_ref[block, :]
+            dq = dq_ref[block, :]
+            rows = jnp.zeros((ROWS, BLOCK), F32)
+            terms = []
+            for h in range(GROUP):
+                p = g * (GROUP // 2) + h // 2
+                lanes = slice((h % 2) * BLOCK, (h % 2 + 1) * BLOCK)
+                cum_t = jnp.broadcast_to(cum_g[:, h : h + 1], (ROWS, BLOCK))
+                decay = jnp.exp2(jnp.minimum(cum_t - cum_rows[h : h + 1, :], 0.0))
+                a = decay * inner_ref[p, block, lanes]
+                step_s = step_rows[h : h + 1, :]
+                ds = ds + a * step_s
+                b = score * a
+                cols[h] = cols[h] + jnp.sum(b.reshape(ROWS // 8, 8, BLOCK), axis=0)
+                w = enter_ref[p, block, lanes] * jnp.exp2(cum_t)
+                dq = dq + w
+                term = b * step_s + w * twice
+                if h in BY_LANES:
+                    total = jnp.sum(term, axis=1, keepdims=True)
+                    rows = jnp.where(lane_index == h, total, rows)
+                else:
+                    high = term.astype(BF16)
+                    terms += [high, (term - high.astype(F32)).astype(BF16)]
+            ds_ref[block, :] = ds
+            dq_ref[block, :] = dq
+            row_groups[g, block, :] = rows + dot(
+                jnp.concatenate(terms, axis=1), pick_ref[...], NN
+            )
+        col_t[pl.ds(at, GROUP), :] = jnp.concatenate(
+            [jnp.sum(part_sum, axis=0, keepdims=True) for part_sum in cols], axis=0
+        )
 
     dcum = row_groups[0]
     for g in range(1, HEADS // GROUP):
@@ -481,6 +507,9 @@
             pltpu.VMEM((HEADS, BLOCK), F32),
             square,
             square,
+            square,
+            square,
+            pltpu.VMEM((2 * (GROUP - len(BY_LANES)) * BLOCK, BLOCK), BF16),
             pltpu.VMEM((COLS, BLOCK), BF16),
             pltpu.VMEM((COLS, NX * NC * BLOCK), BF16),
             pltpu.VMEM((NZ, COLS // NZ, SLICE), BF16),

time: 76.8 us -> 73.5 us (0.957)
  Pallas kernels: 76 us -> 72.7 us
    pallas_call x1, Pallas kernels: 74 us -> 70.6 us  [step(): pl.pallas_call(step_kernel, out_shape=(jax.ShapeDtypeStruct((BLOCK, D), B...]
where the time goes in v4:
time: 73.5 us; the launch traced here: 73.4 us
  Pallas kernels  72.7 us (99%)
    pallas_call x1, Pallas kernels, step(): pl.pallas_call(step_kernel, out_shape=(jax.ShapeDtypeStruct((BLOCK, D), B...  70.6 us
    pallas_call x1, Pallas kernels, outer(): pl.pallas_call(outer_kernel, out_shape=(jax.ShapeDtypeStruct((BLOCK, D),...  2.09 us

profile of v4, /device:TPU:1, one launch (start us, length us, event | category | flops | bytes accessed | tf_op | source)
XLA Modules:
  0.0 73.4 jit_solution(17423859351444669590)
XLA Ops:
  0.6 70.6 %block_step.1 = (bf16[128,4096]{1,0:T(8,128)(2,1)}, f32[8,2,512]{2,1,0:T(2,128)}) custom-call(bf16[128,4096]{1,0:T(8,128)(2,1)} %input_hbm.1, bf16[128,4096]{1,0:T(8,128)(2,1)} %values_hbm.1, bf16[128,4096]{1,0:T(8,128)(2,1)} %cot_hbm.1, bf16[1,64,4096]{2,1,0:T(8,128)(2,1)} %state_hbm.1, f32[1,64]{1,0:T(1,128)} %bitcast.2, f32[1,64]{1,0:T(1,128)} %bitcast.3, ...), custom_call_target="tpu_custom_call" | custom-call | tf_op jit(solution)/shard_map/block_step/pallas_call | solution.py:478
  71.3 2.1 %outer_step.1 = (bf16[128,4096]{1,0:T(8,128)(2,1)}, f32[2,4096]{1,0:T(2,128)}, f32[2,4096]{1,0:T(2,128)}) custom-call(bf16[128,4096]{1,0:T(8,128)(2,1)} %get-tuple-element.5.grad_hbm, f32[8,2,512]{2,1,0:T(2,128)} %get-tuple-element.6.shares_hbm, f32[2,4096]{1,0:T(2,128)} %global_hbm.1, f32[2,4096]{1,0:T(2,128)} %momentum_hbm.1), custom_call_target="tpu_custom_call" | custom-call | tf_op jit(solution)/shard_map/outer_step/pallas_call | solution.py:583

commit v5 on v4

--- a/solution.py
+++ b/solution.py
@@ -143,13 +143,12 @@
     right2 = device(x, yl, yh, shift(z, 2, NZ), c)
     left2 = device(x, yl, yh, shift(z, NZ - 2, NZ), c)
     partner = device(x, yl, yh, z, 1 - c)
-    along_z = [device(x, yl, yh, shift(z, dz, NZ), c) for dz in range(1, NZ)]
     along_y = []
     for dy in range(1, NYL * NYH):
         tyl, tyh = at_y(shift(y, dy, NYL * NYH))
         along_y.append(device(x, tyl, tyh, z, c))
     across = [device(x, yl, shift(yh, dy, NYH), z, 1 - c) for dy in range(1, NYH)]
-    greeted = along_z + along_y + across + replica_group(x, yl, yh, z, c)
+    greeted = [right, right2, left, left2] + along_y + across + replica_group(x, yl, yh, z, c)
     barrier = pltpu.get_barrier_semaphore()
     for target in greeted:
         pl.semaphore_signal(barrier, inc=1, device_id=target, device_id_type=MESH)

time: 73.5 us -> 73.5 us (level)
  no operation moved by 1% of the time
where the time goes in v5:
time: 73.5 us; the launch traced here: 73.3 us
  Pallas kernels  72.7 us (99%)
    pallas_call x1, Pallas kernels, step(): pl.pallas_call(step_kernel, out_shape=(jax.ShapeDtypeStruct((BLOCK, D), B...  70.6 us
    pallas_call x1, Pallas kernels, outer(): pl.pallas_call(outer_kernel, out_shape=(jax.ShapeDtypeStruct((BLOCK, D),...  2.09 us

profile of v5, /device:TPU:1, one launch (start us, length us, event | category | flops | bytes accessed | tf_op | source)
XLA Modules:
  0.0 73.3 jit_solution(17230385803714351058)
XLA Ops:
  0.6 70.6 %block_step.1 = (bf16[128,4096]{1,0:T(8,128)(2,1)}, f32[8,2,512]{2,1,0:T(2,128)}) custom-call(bf16[128,4096]{1,0:T(8,128)(2,1)} %input_hbm.1, bf16[128,4096]{1,0:T(8,128)(2,1)} %values_hbm.1, bf16[128,4096]{1,0:T(8,128)(2,1)} %cot_hbm.1, bf16[1,64,4096]{2,1,0:T(8,128)(2,1)} %state_hbm.1, f32[1,64]{1,0:T(1,128)} %bitcast.2, f32[1,64]{1,0:T(1,128)} %bitcast.3, ...), custom_call_target="tpu_custom_call" | custom-call | tf_op jit(solution)/shard_map/block_step/pallas_call | solution.py:477
  71.2 2.1 %outer_step.1 = (bf16[128,4096]{1,0:T(8,128)(2,1)}, f32[2,4096]{1,0:T(2,128)}, f32[2,4096]{1,0:T(2,128)}) custom-call(bf16[128,4096]{1,0:T(8,128)(2,1)} %get-tuple-element.5.grad_hbm, f32[8,2,512]{2,1,0:T(2,128)} %get-tuple-element.6.shares_hbm, f32[2,4096]{1,0:T(2,128)} %global_hbm.1, f32[2,4096]{1,0:T(2,128)} %momentum_hbm.1), custom_call_target="tpu_custom_call" | custom-call | tf_op jit(solution)/shard_map/outer_step/pallas_call | solution.py:582
